TPU v7x, 512 devices: a whole 4x4x16 slice. The times are simulated.
512 devices in a mesh: seq: 32 (over y, z_lo), mp: 16 (over x, z_hi, core).
Axes of the slice: x: 4, y: 4, z: 16 (z_hi: 2, z_lo: 8; z = z_hi * 8 + z_lo), core: 2. Of those that a mesh axis runs over, the one named last changes fastest.
Arguments:
- tokens: bfloat16 [4096, 8192], P('seq', 'mp'), may hold values from -6 to 6
- in_weight: bfloat16 [8192, 3, 4096], P('seq', None, 'mp'), may hold values from -0.0625 to 0.0625
- short_taps: float32 [3, 3, 4096], P(None, None, 'mp'), may hold values from -4 to 4
- carry_rows: bfloat16 [2, 3, 4096], P(None, None, 'mp'), may hold values from -6 to 6
- pole_rates: float32 [16, 16], replicated, may hold values from 3e-05 to 0.03
- residues: float32 [16, 16], replicated, may hold values from -0.1 to 0.1
- carry_state: float32 [4096, 16], P('mp'), may hold values from -60 to 60
- skip_gain: float32 [4096], P('mp'), may hold values from -4 to 4
- groups: int32 [4096], P('mp'), may hold values from 0 to 15
Outputs:
- result: bfloat16 [4096, 4096], P('seq', 'mp')
All inputs are finite; a program needn't handle non-finite values.
Results may differ from a plain program's by a relative error of at most 0.008.
Values may be sent and summed in bfloat16 or wider, within the bound.
A program may use at most 128 MiB of HBM per device.

v0:
```python
import math
import jax
import jax.numpy as jnp
from jax import lax
from jax.sharding import PartitionSpec as P


def shifted(array, axis, by):
    length = lax.axis_size(axis)
    pairs = [(i, i + by) for i in range(length) if 0 <= i + by < length]
    return lax.ppermute(array, axis, pairs)


def project_rows(source, in_weight, out_width):
    gathered = lax.all_gather(source, "mp", axis=1, tiled=True)
    segment = lax.all_gather(in_weight, "seq", axis=0, tiled=True)
    return jnp.dot(
        gathered, segment.reshape(segment.shape[0], out_width), preferred_element_type=jnp.float32
    )


def channel_modes(chan_groups, pole_rates, residues):
    highest = lax.Precision.HIGHEST
    one_hot = (
        chan_groups[:, None] == jnp.arange(pole_rates.shape[0], dtype=jnp.int32)[None, :]
    ).astype(jnp.float32)
    chan_rates = jnp.dot(one_hot, pole_rates, precision=highest)
    chan_res = jnp.dot(one_hot, residues, precision=highest)
    return (chan_rates, chan_res)


def long_conv(signal, chan_rates, chan_res, chan_state, block_limit):
    highest = lax.Precision.HIGHEST
    chan_count, length = signal.shape
    block_len = math.gcd(length, block_limit)
    block_count = length // block_len
    steps_in = jnp.arange(block_len).astype(jnp.float32)
    decays = jnp.exp(-chan_rates[:, :, None] * steps_in)
    kernel = jnp.sum(chan_res[:, :, None] * decays, axis=1)
    lag_index = jnp.arange(block_len)[:, None] - jnp.arange(block_len)[None, :]
    toeplitz = jnp.where(lag_index >= 0, jnp.take(kernel, jnp.maximum(lag_index, 0), axis=1), 0.0)
    pieces = signal.reshape(chan_count, block_count, block_len)
    inner_part = jnp.einsum("cij,cnj->cni", toeplitz, pieces, precision=highest)
    tail_decay = jnp.exp(-chan_rates[:, :, None] * (block_len - 1.0 - steps_in))
    block_sums = jnp.einsum("crj,cnj->crn", tail_decay, pieces, precision=highest)
    index_blocks = jnp.arange(block_count)
    gap_steps = index_blocks[:, None] - 1 - index_blocks[None, :]
    gap_float = jnp.maximum(gap_steps, 0).astype(jnp.float32) * block_len
    transfer = jnp.where(gap_steps >= 0, jnp.exp(-chan_rates[:, :, None, None] * gap_float), 0.0)
    states = jnp.einsum("crnm,crm->crn", transfer, block_sums, precision=highest)
    start_decay = jnp.exp(-chan_rates[:, :, None] * (index_blocks.astype(jnp.float32) * block_len))
    states = states + start_decay * chan_state[:, :, None]
    lead_decay = chan_res[:, :, None] * jnp.exp(-chan_rates[:, :, None] * (steps_in + 1.0))
    outer_part = jnp.einsum("cri,crn->cni", lead_decay, states, precision=highest)
    return (inner_part + outer_part).reshape(chan_count, length)


def shards(
    tokens, in_weight, short_taps, carry_rows, pole_rates, residues, carry_state, skip_gain, groups
):
    row_count = tokens.shape[0]
    local_width = in_weight.shape[2]
    out_width = 3 * local_width
    is_first = lax.axis_index("seq") == 0
    projected = (
        project_rows(tokens, in_weight, out_width)
        .astype(jnp.bfloat16)
        .reshape(tokens.shape[0], 3, local_width)
    )
    head_rows = shifted(projected[row_count - 2 :], "seq", 1)
    head_rows = jnp.where(is_first, carry_rows, head_rows)
    extended = jnp.concatenate([head_rows, projected], axis=0).astype(jnp.float32)
    short_mix = (
        short_taps[0] * extended[2:]
        + short_taps[1] * extended[1:-1]
        + short_taps[2] * extended[:-2]
    )
    query_rows = short_mix[:, 0]
    gated_rows = (short_mix[:, 1] * short_mix[:, 2]).astype(jnp.bfloat16)
    channel_major = lax.all_to_all(gated_rows.T, "seq", split_axis=0, concat_axis=1, tiled=True)
    chan_count = channel_major.shape[0]
    offset = lax.axis_index("seq") * chan_count
    chan_groups = lax.dynamic_slice_in_dim(groups, offset, chan_count, 0)
    chan_state = lax.dynamic_slice_in_dim(carry_state, offset, chan_count, 0)
    chan_rates, chan_res = channel_modes(chan_groups, pole_rates, residues)
    long_mixed = long_conv(channel_major.astype(jnp.float32), chan_rates, chan_res, chan_state, 256)
    long_rows = lax.all_to_all(
        long_mixed.astype(jnp.bfloat16), "seq", split_axis=1, concat_axis=0, tiled=True
    ).T
    result = query_rows * (
        long_rows.astype(jnp.float32) + skip_gain * gated_rows.astype(jnp.float32)
    )
    return result.astype(jnp.bfloat16)


def solution(mesh):
    in_specs = (
        P("seq", "mp"),
        P("seq", None, "mp"),
        P(None, None, "mp"),
        P(None, None, "mp"),
        P(),
        P(),
        P("mp", None),
        P("mp"),
        P("mp"),
    )
    out_specs = P("seq", "mp")
    return jax.shard_map(shards, mesh=mesh, in_specs=in_specs, out_specs=out_specs, check_vma=False)
```

profile of v0, /device:TPU:4, one launch (start us, length us, event | category | flops | bytes accessed | tf_op | source)
XLA Modules:
  0.0 721.7 jit_solution(1981509274140765477)
XLA Ops:
  6.5 0.0 copy-start
  6.5 0.0 copy-start.6
  6.5 0.0 copy-start.4
  6.5 0.0 copy-start.5
  6.5 0.0 copy-start.1
  6.5 0.0 all-gather.3.cloned.1.call-start
  6.6 0.7 all-gather.3.cloned.1.call-update
  7.3 0.0 all-gather.5.cloned.1.call-start
  7.3 1.9 copy.25
  9.2 0.0 all-gather.5.cloned.1.call-update
  9.3 0.1 copy.37
  9.5 0.0 copy-done.6
  9.5 0.1 dynamic_slice.6
  9.6 0.0 copy-done
  9.6 0.1 constant_dynamic-slice_fusion
  9.6 0.1 maximum_compare_fusion
  9.7 0.0 copy-done.4
  9.7 0.2 convolution_negate_fusion
  9.9 0.0 copy-done.5
  9.9 0.2 fusion.41
  10.1 0.1 multiply_reduce_fusion
  10.2 0.1 fusion.40
  10.3 0.0 copy-done.1
  10.4 93.1 %all-gather.3.cloned.1.call-done = bf16[128,8192]{1,0:T(8,128)(2,1)} async-done(((bf16[128,512]{1,0:T(8,128)(2,1)}), bf16[128,8192]{1,0:T(8,128)(2,1)}) %all-gather.3.cloned.1.call-update) | async-done | bytes 2097168 | tf_op jit(solution)/shard_map/all_gather | solution.py:15
  103.5 316.7 %all-gather.5.cloned.1.call-done = bf16[8192,3,256]{0,2,1:T(8,128)(2,1)} async-done(((bf16[256,3,256]{0,2,1:T(8,128)(2,1)}), bf16[8192,3,256]{0,2,1:T(8,128)(2,1)}) %all-gather.5.cloned.1.call-update) | async-done | bytes 12582928 | tf_op jit(solution)/shard_map/all_gather | solution.py:16
  420.2 0.0 copy-start.2
  420.2 9.5 %convolution_convert_fusion = bf16[128,768]{1,0:T(8,128)(2,1)S(1)} fusion(bf16[128,8192]{1,0:T(8,128)(2,1)} %all-gather.3.cloned.1.call-done, bf16[8192,768]{0,1:T(8,128)(2,1)} %bitcast.52), kind=kOutput, calls=%fused_computation.5 | convolution fusion | flops 1610711040 | bytes 14876672 | tf_op jit(solution)/shard_map/dot_general | solution.py:17
  429.7 1.3 collective-permute-start
  431.0 0.2 copy.27
  431.2 1.1 collective-permute-done
  432.3 0.0 copy-done.2
  432.3 0.2 copy.28
  432.5 0.2 maximum_convert_fusion
  432.7 0.6 fusion.17
  433.3 0.6 fusion.56
  433.9 16.6 %all-to-all-start = ((bf16[32,8,128]{2,1,0:T(8,128)(2,1)}), bf16[32,8,128]{2,1,0:T(8,128)(2,1)S(1)}, u32[]{:S(2)}, u32[]{:S(2)}) async-start(bf16[32,8,128]{2,1,0:T(8,128)(2,1)} %fusion.56), calls=%async_computation | async-start | bytes 131072 | tf_op jit(solution)/shard_map/all_to_all | solution.py:80
  450.5 0.1 copy.30
  450.6 215.6 %gather_fusion = f32[65536,8]{1,0:T(8,128)} fusion(f32[8,256]{0,1:T(8,128)S(1)} %copy.30, s32[65536]{0:T(1024)S(1)} %broadcast_clamp_fusion), kind=kCustom, calls=%fused_computation | custom fusion | bytes 4456448 | tf_op jit(solution)/shard_map/jit(_take)/gather | solution.py:41
  666.3 18.6 %copy.31 = f32[256,256,8]{1,0,2:T(8,128)S(1)} copy(f32[256,256,8]{2,1,0:T(8,128)} %bitcast.51) | data formatting | bytes 4194304 | tf_op jit(solution)/shard_map/jit(_take)/gather | solution.py:41
  684.9 0.1 copy.32
  684.9 0.1 convert_multiply_fusion
  685.0 0.0 all-to-all-done
  685.1 0.3 fusion.26
  685.3 0.0 copy-start.3
  685.4 1.9 fusion.7
  687.3 0.1 copy.36
  687.4 1.3 fusion
  688.7 0.3 fusion.4
  689.1 24.9 %all_to_all.26 = bf16[8,32,128]{2,0,1:T(8,128)(2,1)S(1)} all-to-all(bf16[8,32,128]{2,0,1:T(8,128)(2,1)S(1)} %copy.33), channel_id=1, replica_groups=mesh['seq'=32,'mp'=16] {'seq'}, dimensions={1} | all-to-all | bytes 131072 | tf_op jit(solution)/shard_map/all_to_all | solution.py:87
  714.0 0.0 copy-done.3
  714.0 0.1 fusion.22
  714.1 0.7 copy.34
  (15 shorter events, 0.2 us)
Async XLA Ops:
  6.5 3.0 copy-start
  6.5 2.9 copy-start.6
  6.5 3.2 copy-start.4
  6.5 3.4 copy-start.5
  6.5 3.8 copy-start.1
  6.5 96.9 %all-gather.3.cloned.1.call-start = ((), (), s32[]{:S(2)}) async-start(), calls=%async_computation.2 | async-start | bytes 2228224 | tf_op jit(solution)/shard_map/all_gather | solution.py:15
  7.3 412.9 %all-gather.5.cloned.1.call-start = ((), (), s32[]{:S(2)}) async-start(), calls=%async_computation.3 | async-start | bytes 12976128 | tf_op jit(solution)/shard_map/all_gather | solution.py:16
  420.2 12.1 %copy-start.2 = (bf16[2,3,256]{2,0,1:T(2,128)(2,1)S(1)}, bf16[2,3,256]{2,0,1:T(2,128)(2,1)}, u32[]{:S(2)}) copy-start(bf16[2,3,256]{2,0,1:T(2,128)(2,1)} %param.12) | copy-start | bytes 9220
  429.7 2.6 collective-permute-start
  433.9 251.1 %all-to-all-start = ((bf16[32,8,128]{2,1,0:T(8,128)(2,1)}), bf16[32,8,128]{2,1,0:T(8,128)(2,1)S(1)}, u32[]{:S(2)}, u32[]{:S(2)}) async-start(bf16[32,8,128]{2,1,0:T(8,128)(2,1)} %fusion.56), calls=%async_computation | async-start | bytes 131072 | tf_op jit(solution)/shard_map/all_to_all | solution.py:80
  685.3 28.7 %copy-start.3 = (f32[256]{0:T(256)S(1)}, f32[256]{0:T(256)}, u32[]{:S(2)}) copy-start(f32[256]{0:T(256)} %param.16) | copy-start | bytes 3076
Sparse Core Ops, SparseCore 0:
  10.5 92.9 all-gather.2
  105.5 314.6 all-gather.4
where the time goes:
time: 722 us
  waiting for transfers between devices  412 us (57%)
  local copies, waits for them, and re-layouts  238 us (33%)
  blocking collectives  24.9 us (3%)
  starting transfers between devices  17.9 us (2%)
  matrix products  13.7 us (2%)
  between operations  13.6 us (2%)
    all_gather x1, waiting for transfers between devices, project_rows(): segment = lax.all_gather(in_weight, 'seq', axis=0, tiled=True)  317 us
    gather x2, local copies, waits for them, and re-layouts, long_conv(): jnp.take(kernel, jnp.maximum(lag_index, 0), axis=1)  234 us
    all_gather x1, waiting for transfers between devices, project_rows(): gathered = lax.all_gather(source, 'mp', axis=1, tiled=True)  93.1 us
    all_to_all x1, blocking collectives, shards(): lax.all_to_all(long_mixed.astype(jnp.bfloat16), 'seq', split_axis=1, conc...  24.9 us
    all_to_all x1, starting transfers between devices, shards(): lax.all_to_all(gated_rows.T, 'seq', split_axis=0, concat_axis=1, tiled=True)  16.6 us
  transfers between devices with their start and end apart: 4, of which 3 were waited for; matrix products, arithmetic and copies ran while one was open for 33% of the time, Pallas kernels for 0%

commit v1 on v0

--- a/solution.py
+++ b/solution.py
@@ -13,7 +13,9 @@
 
 def project_rows(source, in_weight, out_width):
     gathered = lax.all_gather(source, "mp", axis=1, tiled=True)
-    segment = lax.all_gather(in_weight, "seq", axis=0, tiled=True)
+    segment = jnp.concatenate(
+        lax.all_to_all(jnp.stack([in_weight] * lax.axis_size("seq")), "seq", 0, 0), axis=0
+    )
     return jnp.dot(
         gathered, segment.reshape(segment.shape[0], out_width), preferred_element_type=jnp.float32
     )

time: 722 us -> 943 us (1.31)
  the two profiles are of different devices: /device:TPU:4 before, /device:TPU:6 now
where the time goes in v1:
time: 943 us; the launch traced here: 942 us
  waiting for transfers between devices  554 us (59%)
  local copies, waits for them, and re-layouts  266 us (28%)
  starting transfers between devices  68.5 us (7%)
  blocking collectives  24.8 us (3%)
  matrix products  13.7 us (1%)
  between operations  13.7 us (1%)
    all_to_all x1, waiting for transfers between devices, project_rows(): lax.all_to_all(jnp.stack([in_weight] * lax.axis_size('seq')), 'seq', 0, 0)  552 us
    gather x2, local copies, waits for them, and re-layouts, long_conv(): jnp.take(kernel, jnp.maximum(lag_index, 0), axis=1)  234 us
    ppermute x1, starting transfers between devices, shifted(): return lax.ppermute(array, axis, pairs)  34.9 us
    all_to_all x1, blocking collectives, shards(): lax.all_to_all(long_mixed.astype(jnp.bfloat16), 'seq', split_axis=1, conc...  24.8 us
  transfers between devices with their start and end apart: 4, of which 2 were waited for; matrix products, arithmetic and copies ran while one was open for 27% of the time, Pallas kernels for 0%

profile of v1, /device:TPU:6, one launch (start us, length us, event | category | flops | bytes accessed | tf_op | source)
XLA Modules:
  0.0 942.4 jit_solution(9719549452755626224)
XLA Ops:
  6.5 0.0 copy-start
  6.5 1.2 copy.26
  7.7 6.0 stack.2
  13.7 0.0 copy-start.7
  13.7 0.0 copy-start.5
  13.7 0.0 copy-start.6
  13.7 0.0 copy-start.2
  13.8 15.8 %all-to-all-start = ((bf16[32,256,3,256]{1,3,2,0:T(8,128)(2,1)}), bf16[32,256,3,256]{1,3,2,0:T(8,128)(2,1)}, u32[]{:S(2)}, u32[]{:S(2)}) async-start(bf16[32,256,3,256]{1,3,2,0:T(8,128)(2,1)} %stack.2), calls=%async_computation | async-start | bytes 25165824 | tf_op jit(solution)/shard_map/all_to_all | solution.py:17
  29.6 0.0 all-gather.2.cloned.1.call-start
  29.6 0.7 all-gather.2.cloned.1.call-update
  30.3 0.1 copy.40
  30.5 0.0 copy-done.7
  30.5 0.1 dynamic_slice.6
  30.6 0.0 copy-done
  30.6 0.1 constant_dynamic-slice_fusion
  30.7 0.1 maximum_compare_fusion
  30.7 0.0 copy-done.5
  30.7 0.2 convolution_negate_fusion
  30.9 0.0 copy-done.6
  30.9 0.2 fusion.41
  31.1 0.1 multiply_reduce_fusion
  31.3 0.1 fusion.40
  31.3 0.0 copy-done.2
  31.4 552.1 %all-to-all-done = bf16[32,256,3,256]{1,3,2,0:T(8,128)(2,1)} async-done(((bf16[32,256,3,256]{1,3,2,0:T(8,128)(2,1)}), bf16[32,256,3,256]{1,3,2,0:T(8,128)(2,1)}, u32[]{:S(2)}, u32[]{:S(2)}) %all-to-all-start) | async-done | bytes 12582944 | tf_op jit(solution)/shard_map/all_to_all | solution.py:17
  583.5 11.9 %copy.27 = bf16[32,256,3,256]{1,0,3,2:T(8,128)(2,1)S(1)} copy(bf16[32,256,3,256]{1,3,2,0:T(8,128)(2,1)} %all-to-all-done) | data formatting | bytes 25165824 | tf_op jit(solution)/shard_map/all_to_all | solution.py:17
  595.4 10.7 %copy.39 = bf16[96,8,32,256]{3,1,2,0:T(8,128)(2,1)} copy(bf16[96,8,32,256]{3,2,1,0:T(8,128)(2,1)S(1)} %bitcast.56) | data formatting | bytes 25165824
  606.2 0.0 all-gather.2.cloned.1.call-done
  606.2 0.0 copy-start.3
  606.2 9.5 %convolution_convert_fusion = bf16[128,768]{1,0:T(8,128)(2,1)S(1)} fusion(bf16[128,8192]{1,0:T(8,128)(2,1)} %all-gather.2.cloned.1.call-done, bf16[8192,768]{0,1:T(8,128)(2,1)} %bitcast.55), kind=kOutput, calls=%fused_computation.5 | convolution fusion | flops 1610711040 | bytes 14876672 | tf_op jit(solution)/shard_map/dot_general | solution.py:19
  615.7 34.9 %collective-permute-start = (bf16[2,3,256]{2,1,0:T(4,128)(2,1)S(1)}, bf16[2,3,256]{2,1,0:T(4,128)(2,1)S(1)}, u32[]{:S(2)}, u32[]{:S(2)}) collective-permute-start(bf16[2,3,256]{2,1,0:T(4,128)(2,1)S(1)} %slice.35), channel_id=1, source_target_pairs={{0,16},{16,32},{32,48},{48,64},{64,80},{80,96},{96,112},{112,128},... | collective-permute-start | bytes 9224 | tf_op jit(solution)/shard_map/ppermute | solution.py:11
  650.6 0.2 copy.29
  650.8 1.1 collective-permute-done
  651.9 0.0 copy-done.3
  651.9 0.2 copy.30
  652.1 0.2 maximum_convert_fusion
  652.3 0.6 fusion.17
  652.9 0.6 fusion.56
  653.5 17.8 %all-to-all-start.1 = ((bf16[32,8,128]{2,1,0:T(8,128)(2,1)}), bf16[32,8,128]{2,1,0:T(8,128)(2,1)S(1)}, u32[]{:S(2)}, u32[]{:S(2)}) async-start(bf16[32,8,128]{2,1,0:T(8,128)(2,1)} %fusion.56), calls=%async_computation.1 | async-start | bytes 131072 | tf_op jit(solution)/shard_map/all_to_all | solution.py:82
  671.3 0.1 copy.32
  671.5 215.6 %gather_fusion = f32[65536,8]{1,0:T(8,128)} fusion(f32[8,256]{0,1:T(8,128)S(1)} %copy.32, s32[65536]{0:T(1024)S(1)} %broadcast_clamp_fusion), kind=kCustom, calls=%fused_computation | custom fusion | bytes 4456448 | tf_op jit(solution)/shard_map/jit(_take)/gather | solution.py:43
  887.1 18.6 %copy.33 = f32[256,256,8]{1,0,2:T(8,128)S(1)} copy(f32[256,256,8]{2,1,0:T(8,128)} %bitcast.57) | data formatting | bytes 4194304 | tf_op jit(solution)/shard_map/jit(_take)/gather | solution.py:43
  905.7 0.1 copy.34
  905.8 0.1 convert_multiply_fusion
  905.8 0.0 all-to-all-done.1
  905.9 0.3 fusion.26
  906.2 0.0 copy-start.4
  906.2 0.0 copy-start.1
  906.2 1.9 fusion.7
  908.1 0.1 copy.38
  908.2 1.3 fusion
  909.5 0.3 fusion.4
  909.9 24.8 %all_to_all.31 = bf16[8,32,128]{2,0,1:T(8,128)(2,1)S(1)} all-to-all(bf16[8,32,128]{2,0,1:T(8,128)(2,1)S(1)} %copy.35), channel_id=1, replica_groups=mesh['seq'=32,'mp'=16] {'seq'}, dimensions={1} | all-to-all | bytes 131072 | tf_op jit(solution)/shard_map/all_to_all | solution.py:89
  934.7 0.0 copy-done.4
  934.7 0.1 fusion.22
  934.8 0.7 copy.36
  935.5 0.0 copy-done.1
  (15 shorter events, 0.2 us)
Async XLA Ops:
  6.5 24.1 %copy-start = (f32[256,16]{0,1:T(8,128)S(1)}, f32[256,16]{0,1:T(8,128)}, u32[]{:S(2)}) copy-start(f32[256,16]{0,1:T(8,128)} %param.15) | copy-start | bytes 49156
  13.7 16.7 %copy-start.7 = (s32[256]{0:T(256)S(1)}, s32[256]{0:T(256)}, u32[]{:S(2)}) copy-start(s32[256]{0:T(256)} %param.17) | copy-start | bytes 3076
  13.7 17.0 %copy-start.5 = (f32[16,16]{1,0:T(8,128)S(1)}, f32[16,16]{1,0:T(8,128)}, u32[]{:S(2)}) copy-start(f32[16,16]{1,0:T(8,128)} %param.13) | copy-start | bytes 3076
  13.7 17.2 %copy-start.6 = (f32[16,16]{1,0:T(8,128)S(1)}, f32[16,16]{1,0:T(8,128)}, u32[]{:S(2)}) copy-start(f32[16,16]{1,0:T(8,128)} %param.14) | copy-start | bytes 3076
  13.7 17.6 %copy-start.2 = (f32[3,3,256]{2,1,0:T(4,128)S(1)}, f32[3,3,256]{2,1,0:T(4,128)}, u32[]{:S(2)}) copy-start(f32[3,3,256]{2,1,0:T(4,128)} %param.11) | copy-start | bytes 27652
  13.8 569.8 %all-to-all-start = ((bf16[32,256,3,256]{1,3,2,0:T(8,128)(2,1)}), bf16[32,256,3,256]{1,3,2,0:T(8,128)(2,1)}, u32[]{:S(2)}, u32[]{:S(2)}) async-start(bf16[32,256,3,256]{1,3,2,0:T(8,128)(2,1)} %stack.2), calls=%async_computation | async-start | bytes 25165824 | tf_op jit(solution)/shard_map/all_to_all | solution.py:17
  29.6 576.6 %all-gather.2.cloned.1.call-start = ((), (), s32[]{:S(2)}) async-start(), calls=%async_computation.3 | async-start | bytes 2228224 | tf_op jit(solution)/shard_map/all_gather | solution.py:15
  606.2 45.8 %copy-start.3 = (bf16[2,3,256]{2,0,1:T(2,128)(2,1)S(1)}, bf16[2,3,256]{2,0,1:T(2,128)(2,1)}, u32[]{:S(2)}) copy-start(bf16[2,3,256]{2,0,1:T(2,128)(2,1)} %param.12) | copy-start | bytes 9220
  615.7 36.2 %collective-permute-start = (bf16[2,3,256]{2,1,0:T(4,128)(2,1)S(1)}, bf16[2,3,256]{2,1,0:T(4,128)(2,1)S(1)}, u32[]{:S(2)}, u32[]{:S(2)}) collective-permute-start(bf16[2,3,256]{2,1,0:T(4,128)(2,1)S(1)} %slice.35), channel_id=1, source_target_pairs={{0,16},{16,32},{32,48},{48,64},{64,80},{80,96},{96,112},{112,128},... | collective-permute-start | bytes 9224 | tf_op jit(solution)/shard_map/ppermute | solution.py:11
  653.5 252.3 %all-to-all-start.1 = ((bf16[32,8,128]{2,1,0:T(8,128)(2,1)}), bf16[32,8,128]{2,1,0:T(8,128)(2,1)S(1)}, u32[]{:S(2)}, u32[]{:S(2)}) async-start(bf16[32,8,128]{2,1,0:T(8,128)(2,1)} %fusion.56), calls=%async_computation.1 | async-start | bytes 131072 | tf_op jit(solution)/shard_map/all_to_all | solution.py:82
  906.2 28.5 %copy-start.4 = (f32[256]{0:T(256)S(1)}, f32[256]{0:T(256)}, u32[]{:S(2)}) copy-start(f32[256]{0:T(256)} %param.16) | copy-start | bytes 3076
  906.2 29.4 %copy-start.1 = (f32[256,16]{0,1:T(8,128)S(1)}, f32[256,16]{0,1:T(8,128)}, u32[]{:S(2)}) copy-start(f32[256,16]{0,1:T(8,128)} %param.15) | copy-start | bytes 49156
Sparse Core Ops, SparseCore 0:
  33.5 187.0 all-gather.1
